TPU v7x, 32 devices: a whole 2x2x4 slice. The times are simulated.
32 devices in a mesh: groups: 2 (over x), vel: 16 (over z, y, core).
Axes of the slice: x: 2, y: 2, z: 4, core: 2. Of those that a mesh axis runs over, the one named last changes fastest.
Arguments:
- epoch_maps: bfloat16 [128, 192, 512], P('vel', 'groups'), parts along dimension 1, may hold values from -6 to 6, as said below
- velocity: int32 [16, 2], P('vel'), may hold values from -16 to 16, as said below
- slot_epoch: int32 [64], replicated, may hold values from 0 to 63, each once
- epoch_time: int32 [64], replicated, may hold values from 0 to 127, as said below
Outputs:
- likelihood: float32 [16, 192, 512], P('vel', 'groups'), parts along dimension 1
- best_value: float32 [192, 512], P('groups'), parts along dimension 0
There are 2 independent parts, one for each index of `groups`. A program takes and returns all parts, laid end to end along the dimension named above; an argument that names none is the same for every part. Nothing has to cross between parts.
Inputs may be any that keep to these rules, and one draw needn't show every extreme that they name: `epoch_maps`: the first 64 images are likelihoods, the others weights of at least 0.25 and at most 4. `velocity`: all rows are distinct; rows (16, 16) and (-16, -16) both occur. `epoch_time`: strictly increasing, the first 0 and the last 127. `slot_epoch`: each epoch stands in exactly one slot.
All inputs are finite; a program needn't handle non-finite values.
Results may differ from a plain program's by a relative error of at most 0.0029.
Values may be sent and summed in bfloat16 or wider, within the bound.
A program may use at most 64 MiB of HBM per device.

v0:
```python
import functools
import math

import jax
import jax.numpy as jnp
from jax import lax
from jax.experimental import pallas as pl
from jax.experimental.pallas import tpu as pltpu
from jax.sharding import PartitionSpec as P

SPLINE = (
    (64.0, 256.0, 64.0, 0.0),
    (27.0, 235.0, 121.0, 1.0),
    (8.0, 184.0, 184.0, 8.0),
    (1.0, 121.0, 235.0, 27.0),
)
spline_norm = 147456.0
rate_divisor = 32
HALO = 64
LANES = 128


def scalar_taps(offset):
    whole = offset >> 2
    fraction = offset & 3
    taps = []
    for tap in range(4):
        value = jnp.float32(SPLINE[3][tap])
        for level in range(3):
            value = jnp.where(fraction == level, jnp.float32(SPLINE[level][tap]), value)
        taps.append(value)
    return whole, taps


def band(distance, offset):
    whole, taps = scalar_taps(offset)
    relative = distance - whole
    out = jnp.where(relative == 3, taps[3], 0.0)
    for tap in (2, 1, 0):
        out = jnp.where(relative == tap, taps[tap], out)
    return out.astype(jnp.bfloat16)


def stack_one(rate_row, rate_col, times, padded, bands, rows_done, count, rows, cols):
    blocks = cols // LANES
    row_distance = (
        lax.broadcasted_iota(jnp.int32, (rows, rows), 1)
        - lax.broadcasted_iota(jnp.int32, (rows, rows), 0)
        + 1
    )
    col_distance = (
        lax.broadcasted_iota(jnp.int32, (2 * LANES, LANES), 0)
        - lax.broadcasted_iota(jnp.int32, (2 * LANES, LANES), 1)
        + (1 - HALO)
    )
    for s in range(count):
        row_band = band(row_distance, (rate_row * times(s)) >> 5)
        bands[pl.ds(s * 2 * LANES, 2 * LANES), :] = band(
            col_distance, (rate_col * times(s)) >> 5
        )
        rows_done[s] = jnp.dot(
            row_band, padded[s], preferred_element_type=jnp.float32
        ).astype(jnp.bfloat16)
    lhs = jnp.concatenate(
        [
            jnp.concatenate(
                [rows_done[s, :, b * LANES : (b + 2) * LANES] for s in range(count)], axis=1
            )
            for b in range(blocks)
        ],
        axis=0,
    )
    return jnp.dot(lhs, bands[...], preferred_element_type=jnp.float32)


def pad_images(images, padded, start, count):
    zeros = jnp.zeros((images.shape[1], HALO), jnp.bfloat16)
    for s in range(count):
        padded[start + s] = jnp.concatenate([zeros, images[s], zeros], axis=1)


def stack_kernel(count, rows, cols, vel_ref, time_ref, images, out, padded, bands, rows_done):
    pad_images(images, padded, 0, count)
    hypotheses = out.shape[0]

    @pl.loop(0, hypotheses)
    def _(v):
        total = stack_one(
            vel_ref[v, 0],
            vel_ref[v, 1],
            lambda s: time_ref[s],
            padded,
            bands,
            rows_done,
            count,
            rows,
            cols,
        )
        for b in range(cols // LANES):
            out[v, :, b * LANES : (b + 1) * LANES] = total[b * rows : (b + 1) * rows].astype(
                out.dtype
            )


def fused_kernel(
    chips,
    epochs,
    count,
    rows,
    cols,
    se_ref,
    et_ref,
    vel_ref,
    images,
    out_ref,
    peer_images,
    padded,
    bands,
    rows_done,
    vel_all,
    part_send,
    part_recv,
    far_own,
    hop_recv,
    far_send,
    like_send,
    max_send,
    max_recv,
    best_send,
    image_sems,
    vel_send,
    vel_recv,
    part_ssem,
    part_rsem,
    hop_ssem,
    hop_rsem,
    max_sems,
    like_ssem,
    like_rsem,
    best_ssem,
    best_rsem,
):
    like_out, best_out = out_ref.at[pl.ds(0, 1)], out_ref.at[1]
    me = lax.axis_index("vel")
    chip, core = me // 2, me % 2
    sibling = chip * 2 + 1 - core
    blocks = cols // LANES
    half, quarter = chips // 2, chips // 4
    slice_rows = rows * blocks // chips
    near0 = chip // half * half
    far0 = half - near0
    group = chip // quarter
    inner = (group + 1) // 2 % 2
    partner = chip + quarter * (1 - 2 * (group % 2))
    far_inner = quarter * (2 - chip // half)

    def window(owner):
        return (
            pl.ds(pl.multiple_of(owner // blocks * slice_rows, slice_rows), slice_rows),
            pl.ds(pl.multiple_of(owner % blocks * LANES, LANES), LANES),
        )

    def remote(source, target, send, receive, device):
        return pltpu.make_async_remote_copy(
            src_ref=source,
            dst_ref=target,
            send_sem=send,
            recv_sem=receive,
            device_id={"vel": device},
            device_id_type=pl.DeviceIdType.MESH,
        )

    def rail(other):
        return other * 2 + core

    def each_rail(body):
        @pl.loop(1, chips)
        def _(step):
            body(lax.rem(chip + step, chips))

    def each_near(body):
        @pl.loop(1, half)
        def _(step):
            body(near0 + lax.rem(chip - near0 + step, half))

    def greet(device):
        pl.semaphore_signal(
            barrier, inc=1, device_id={"vel": device}, device_id_type=pl.DeviceIdType.MESH
        )

    barrier = pltpu.get_barrier_semaphore()
    greet(sibling)
    each_rail(lambda other: greet(rail(other)))
    pad_images(images, padded, 0, count)
    max_send[...] = jnp.full_like(max_send, -jnp.inf)
    pl.semaphore_wait(barrier, chips)

    def vel_copy(source, target, other):
        return remote(vel_ref, vel_all.at[target], vel_send.at[source], vel_recv.at[target], rail(other))

    each_rail(lambda other: vel_copy(other, chip, other).start())
    swap = remote(images, peer_images, image_sems.at[0], image_sems.at[1], sibling)
    swap.start()
    vel_all[chip, 0, 0] = vel_ref[0, 0]
    vel_all[chip, 0, 1] = vel_ref[0, 1]
    swap.wait_recv()
    pad_images(peer_images, padded, count, count)
    each_rail(lambda other: vel_copy(other, other, other).wait())

    first = lax.rem(me * count, epochs)
    peer_first = lax.rem(sibling * count, epochs)

    def time(s):
        slot = first + s if s < count else peer_first + (s - count)
        return et_ref[se_ref[slot]]

    def part_copy(v, source, other):
        return remote(
            part_send.at[v, other],
            part_recv.at[v, source],
            part_ssem.at[v, other],
            part_rsem.at[v, source],
            rail(other),
        )

    def far_copy(v, step, source):
        other = far0 + step
        return remote(
            far_send.at[v, step],
            part_recv.at[v, source],
            part_ssem.at[v, other],
            part_rsem.at[v, source],
            rail(other),
        )

    def hop_copy(v):
        return remote(
            part_send.at[v, pl.ds(far0, half)],
            hop_recv.at[v],
            hop_ssem.at[v],
            hop_rsem.at[v],
            rail(partner),
        )

    def like_copy(v, owner):
        return remote(
            like_send.at[v],
            like_out.at[0, window(owner)[0], window(owner)[1]],
            like_ssem.at[v],
            like_rsem.at[owner],
            rail(v),
        )

    def forward(v):
        @pl.when(inner == 1)
        def _():
            hop_copy(v).wait_recv()

            @pl.loop(0, half)
            def _(step):
                total = far_own[v % 2, far0 + step] + hop_recv[v, step].astype(jnp.float32)
                far_send[v, step] = total.astype(jnp.bfloat16)
                far_copy(v, step, chip).start()

    def finish_like(v):
        each_near(lambda other: part_copy(v, other, other).wait_recv())

        @pl.loop(0, quarter)
        def _(step):
            far_copy(v, 0, far_inner + step).wait_recv()

        near = part_recv[v, near0].astype(jnp.float32)
        for step in range(1, half):
            near = near + part_recv[v, near0 + step].astype(jnp.float32)
        far = part_recv[v, far_inner].astype(jnp.float32)
        for step in range(1, quarter):
            far = far + part_recv[v, far_inner + step].astype(jnp.float32)
        first_kind = near0 == 0
        signal = jnp.where(first_kind, near, far) / spline_norm
        weight = jnp.where(first_kind, far, near) / spline_norm
        value = signal / jnp.sqrt(weight + 1.0)
        max_send[...] = jnp.maximum(max_send[...], value)
        like_send[v] = value

        @pl.when(v != chip)
        def _():
            like_copy(v, chip).start()

    late = 3

    @pl.loop(0, chips)
    def _(v):
        total = stack_one(
            vel_all[v, 0, 0],
            vel_all[v, 0, 1],
            time,
            padded,
            bands,
            rows_done,
            2 * count,
            rows,
            cols,
        )
        for t in range(chips):
            start = t % blocks * rows + t // blocks * slice_rows
            piece = total[start : start + slice_rows]
            far_own[v % 2, t] = piece
            part_send[v, t] = piece.astype(jnp.bfloat16)
        part_recv[v, chip] = part_send[v, chip]

        @pl.when(inner == 0)
        def _():
            hop_copy(v).start()

        each_near(lambda other: part_copy(v, chip, other).start())

        @pl.when(v >= 1)
        def _():
            forward(v - 1)

        @pl.when(v >= late)
        def _():
            finish_like(v - late)

    forward(chips - 1)

    @pl.loop(chips - late, chips)
    def _(v):
        finish_like(v)

    meet = remote(max_send, max_recv, max_sems.at[0], max_sems.at[1], sibling)
    meet.start()
    like_out[0, window(chip)[0], window(chip)[1]] = like_send[chip]
    meet.wait()
    best_send[...] = jnp.maximum(max_send[...], max_recv[...])

    def best_copy(owner, other):
        return remote(
            best_send,
            best_out.at[window(owner)[0], window(owner)[1]],
            best_ssem.at[other],
            best_rsem.at[owner],
            rail(other),
        )

    each_rail(lambda other: best_copy(chip, other).start())
    best_out[window(chip)[0], window(chip)[1]] = best_send[...]

    @pl.loop(0, chips)
    def _(v):
        each_near(lambda other: part_copy(v, chip, other).wait_send())

        @pl.when(inner == 0)
        def _():
            hop_copy(v).wait_send()

        @pl.when(inner == 1)
        def _():
            @pl.loop(0, half)
            def _(step):
                far_copy(v, step, chip).wait_send()

    swap.wait_send()

    def finish(other):
        like_copy(other, other).wait()
        best_copy(other, other).wait()

    each_rail(finish)


def fused(n, epoch_maps, velocity, slot_epoch, epoch_time):
    count, rows, cols = epoch_maps.shape
    epochs = slot_epoch.shape[0]
    chips = n // 2
    half = chips // 2
    slice_rows = rows * (cols // LANES) // chips
    smem = pl.BlockSpec(memory_space=pltpu.SMEM)
    vmem = pl.BlockSpec(memory_space=pltpu.VMEM)
    f32, bf16 = jnp.float32, jnp.bfloat16
    dma = pltpu.SemaphoreType.DMA
    both = pl.pallas_call(
        functools.partial(fused_kernel, chips, epochs, count, rows, cols),
        out_shape=jax.ShapeDtypeStruct((2, rows, cols), f32),
        in_specs=[smem, smem, smem, vmem],
        out_specs=vmem,
        scratch_shapes=[
            pltpu.VMEM((count, rows, cols), bf16),
            pltpu.VMEM((2 * count, rows, cols + 2 * HALO), bf16),
            pltpu.VMEM((2 * count * 2 * LANES, LANES), bf16),
            pltpu.VMEM((2 * count, rows, cols + 2 * HALO), bf16),
            pltpu.SMEM((chips, 1, 2), jnp.int32),
            pltpu.VMEM((chips, chips, slice_rows, LANES), bf16),
            pltpu.VMEM((chips, chips, slice_rows, LANES), bf16),
            pltpu.VMEM((2, chips, slice_rows, LANES), f32),
            pltpu.VMEM((chips, half, slice_rows, LANES), bf16),
            pltpu.VMEM((chips, half, slice_rows, LANES), bf16),
            pltpu.VMEM((chips, slice_rows, LANES), f32),
            pltpu.VMEM((slice_rows, LANES), f32),
            pltpu.VMEM((slice_rows, LANES), f32),
            pltpu.VMEM((slice_rows, LANES), f32),
            dma((2,)),
            dma((chips,)),
            dma((chips,)),
            dma((chips, chips)),
            dma((chips, chips)),
            dma((chips,)),
            dma((chips,)),
            dma((2,)),
            dma((chips,)),
            dma((chips,)),
            dma((chips,)),
            dma((chips,)),
        ],
        compiler_params=pltpu.CompilerParams(collective_id=0, has_side_effects=True),
    )(slot_epoch, epoch_time, velocity, epoch_maps)
    return (both[:1], both[1])


def fits(n, epoch_maps, velocity, epochs):
    count, rows, cols = epoch_maps.shape
    chips = n // 2
    blocks = cols // LANES
    return (
        n % 4 == 0
        and velocity.shape[0] == 1
        and n * count == 2 * epochs
        and cols % LANES == 0
        and chips % blocks == 0
        and rows % (chips // blocks * 16) == 0
    )


def local(n, epoch_maps, velocity, slot_epoch, epoch_time):
    count, rows, cols = epoch_maps.shape
    epochs = slot_epoch.shape[0]
    if fits(n, epoch_maps, velocity, epochs):
        return fused(n, epoch_maps, velocity, slot_epoch, epoch_time)
    me = lax.axis_index("vel")
    vels = lax.all_gather(velocity, "vel", axis=0, tiled=True)
    first = lax.rem(me * count, epochs)
    slots = lax.dynamic_slice_in_dim(slot_epoch, first, count, 0)
    times = epoch_time[slots]
    partial = pl.pallas_call(
        functools.partial(stack_kernel, count, rows, cols),
        out_shape=jax.ShapeDtypeStruct((vels.shape[0], rows, cols), jnp.bfloat16),
        in_specs=[
            pl.BlockSpec(memory_space=pltpu.SMEM),
            pl.BlockSpec(memory_space=pltpu.SMEM),
            pl.BlockSpec(memory_space=pltpu.VMEM),
        ],
        out_specs=pl.BlockSpec(memory_space=pltpu.VMEM),
        scratch_shapes=[
            pltpu.VMEM((count, rows, cols + 2 * HALO), jnp.bfloat16),
            pltpu.VMEM((count * 2 * LANES, LANES), jnp.bfloat16),
            pltpu.VMEM((count, rows, cols + 2 * HALO), jnp.bfloat16),
        ],
    )(vels, times, epoch_maps)
    mine = velocity.shape[0]
    received = lax.all_to_all(partial, "vel", 0, 0, tiled=True)
    received = received.reshape(2, n // 2, mine, rows, cols)
    stack_sums = jnp.sum(received.astype(jnp.float32), axis=1) / spline_norm
    likelihood = stack_sums[0] / jnp.sqrt(stack_sums[1] + 1.0)
    best_value = lax.pmax(jnp.max(likelihood, axis=0), "vel")
    return (likelihood, best_value)


def solution(mesh):
    return jax.shard_map(
        functools.partial(local, mesh.shape["vel"]),
        mesh=mesh,
        in_specs=(P("vel", "groups", None), P("vel", None), P(), P()),
        out_specs=(P("vel", "groups", None), P("groups", None)),
        check_vma=False,
    )
```

profile of v0, /device:TPU:0, one launch (start us, length us, event | category | flops | bytes accessed | tf_op | source)
XLA Modules:
  0.0 45.6 jit_solution(9606200665834610048)
XLA Ops:
  0.6 43.2 %shard_map.59 = f32[2,96,512]{2,1,0:T(8,128)} custom-call(s32[64]{0:T(128)} %se_ref.1, s32[64]{0:T(128)} %et_ref.1, s32[1,2]{1,0:T(1,128)} %vel_ref.1, bf16[8,96,512]{2,1,0:T(8,128)(2,1)} %images.1), custom_call_target="tpu_custom_call" | custom-call | tf_op jit(solution)/shard_map/pallas_call | solution.py:382
  43.8 1.8 %slice_bitcast_fusion = (f32[96,512]{1,0:T(8,128)}, f32[1,96,512]{2,1,0:T(8,128)}) fusion(f32[2,96,512]{2,1,0:T(8,128)} %shard_map.59), kind=kLoop, calls=%fused_computation | loop fusion | bytes 786432 | tf_op jit(solution)/shard_map/squeeze | solution.py:417
where the time goes:
time: 45.7 us; the launch traced here: 45.6 us
  Pallas kernels  43.2 us (95%)
  local copies, waits for them, and re-layouts  1.79 us (4%)
  between operations  0.64 us (1%)
    pallas_call x1, Pallas kernels, fused(): pl.pallas_call(functools.partial(fused_kernel, chips, epochs, count, rows...  43.2 us
    squeeze x1, local copies, waits for them, and re-layouts, fused(): return (both[:1], both[1])  1.79 us

commit v1 on v0

--- a/solution.py
+++ b/solution.py
@@ -18,6 +18,10 @@
 rate_divisor = 32
 HALO = 64
 LANES = 128
+REACH = 16
+EDGE = 8
+FORWARD_LAG = 3
+LIKE_LAG = 6
 
 
 def scalar_taps(offset):
@@ -102,6 +106,14 @@
             )
 
 
+def tap_select(relative, taps):
+    out = jnp.zeros(relative.shape, jnp.float32)
+    for tap in range(4):
+        if taps[tap]:
+            out = jnp.where(relative == tap, jnp.float32(taps[tap]), out)
+    return out
+
+
 def fused_kernel(
     chips,
     epochs,
@@ -114,9 +126,11 @@
     images,
     out_ref,
     peer_images,
-    padded,
+    row_taps,
+    table,
+    base,
+    lhs,
     bands,
-    rows_done,
     vel_all,
     part_send,
     part_recv,
@@ -145,20 +159,23 @@
     chip, core = me // 2, me % 2
     sibling = chip * 2 + 1 - core
     blocks = cols // LANES
-    half, quarter = chips // 2, chips // 4
+    levels, near_levels = chips // 2, chips // 4
+    half = chips // 2
     slice_rows = rows * blocks // chips
-    near0 = chip // half * half
-    far0 = half - near0
-    group = chip // quarter
-    inner = (group + 1) // 2 % 2
-    partner = chip + quarter * (1 - 2 * (group % 2))
-    far_inner = quarter * (2 - chip // half)
+    level, column = chip // 2, chip % 2
+    mate = level * 2 + 1 - column
+    near0 = level // near_levels * half
+    far_level = near_levels - level // near_levels * near_levels
+    images_all = 2 * count
 
     def window(owner):
         return (
             pl.ds(pl.multiple_of(owner // blocks * slice_rows, slice_rows), slice_rows),
             pl.ds(pl.multiple_of(owner % blocks * LANES, LANES), LANES),
         )
+
+    def slot(owner):
+        return owner % 2 * levels + owner // 2
 
     def remote(source, target, send, receive, device):
         return pltpu.make_async_remote_copy(
@@ -191,32 +208,100 @@
     barrier = pltpu.get_barrier_semaphore()
     greet(sibling)
     each_rail(lambda other: greet(rail(other)))
-    pad_images(images, padded, 0, count)
+
+    span = rows + 2 * EDGE
+    relative = (
+        lax.broadcasted_iota(jnp.int32, (span, rows), 1)
+        - lax.broadcasted_iota(jnp.int32, (span, rows), 0)
+        + (EDGE + 1)
+    )
+    for f in range(4):
+        row_taps[f * span : (f + 1) * span, :] = tap_select(relative, SPLINE[f]).astype(jnp.bfloat16)
+    base_shape = base.shape[2:]
+    for h in range(2):
+        distance = (
+            lax.broadcasted_iota(jnp.int32, base_shape, 0)
+            - lax.broadcasted_iota(jnp.int32, base_shape, 1)
+            + (HALO + 1 - REACH - h * LANES)
+        )
+        for f in range(4):
+            base[f, h] = tap_select(distance, SPLINE[f])
+    blank = jnp.zeros((blocks, REACH - EDGE, LANES), jnp.float32)
+
+    def filter_rows(source, s, index):
+        mixed = jnp.dot(row_taps[...], source[s], preferred_element_type=jnp.float32)
+        mixed = mixed.astype(jnp.bfloat16).astype(jnp.float32)
+        for f in range(4):
+            table[index * 4 + f, :, 0 : REACH - EDGE] = blank
+            table[index * 4 + f, :, REACH + rows + EDGE : rows + 2 * REACH] = blank
+            for b in range(blocks):
+                table[index * 4 + f, b, REACH - EDGE : REACH + rows + EDGE] = mixed[
+                    f * span : (f + 1) * span, b * LANES : (b + 1) * LANES
+                ]
+
+    early = count // 2
+
+    @pl.loop(0, early)
+    def _(s):
+        filter_rows(images, s, s)
+
     max_send[...] = jnp.full_like(max_send, -jnp.inf)
     pl.semaphore_wait(barrier, chips)
 
     def vel_copy(source, target, other):
         return remote(vel_ref, vel_all.at[target], vel_send.at[source], vel_recv.at[target], rail(other))
 
-    each_rail(lambda other: vel_copy(other, chip, other).start())
     swap = remote(images, peer_images, image_sems.at[0], image_sems.at[1], sibling)
     swap.start()
+    each_rail(lambda other: vel_copy(other, chip, other).start())
     vel_all[chip, 0, 0] = vel_ref[0, 0]
     vel_all[chip, 0, 1] = vel_ref[0, 1]
+
+    @pl.loop(early, count)
+    def _(s):
+        filter_rows(images, s, s)
+
     swap.wait_recv()
-    pad_images(peer_images, padded, count, count)
-    each_rail(lambda other: vel_copy(other, other, other).wait())
+
+    @pl.loop(0, count)
+    def _(s):
+        filter_rows(peer_images, s, s + count)
 
     first = lax.rem(me * count, epochs)
     peer_first = lax.rem(sibling * count, epochs)
 
     def time(s):
-        slot = first + s if s < count else peer_first + (s - count)
-        return et_ref[se_ref[slot]]
+        at = first + s if s < count else peer_first + (s - count)
+        return et_ref[se_ref[at]]
+
+    def stack(rate_row, rate_col):
+        for s in range(images_all):
+            qr = (rate_row * time(s)) >> 5
+            qc = (rate_col * time(s)) >> 5
+            for b in range(blocks):
+                lhs[b * rows : (b + 1) * rows, s * LANES : (s + 1) * LANES] = table[
+                    s * 4 + (qr & 3), b, pl.ds((qr >> 2) + REACH, rows), :
+                ].astype(jnp.bfloat16)
+            for h in range(2):
+                bands[s * LANES : (s + 1) * LANES, h * LANES : (h + 1) * LANES] = base[
+                    qc & 3, h, pl.ds(REACH - (qc >> 2), LANES), :
+                ].astype(jnp.bfloat16)
+        wide = jnp.dot(lhs[...], bands[...], preferred_element_type=jnp.float32)
+        tiles = []
+        for t in range(blocks + 1):
+            tile = None
+            if t < blocks:
+                tile = wide[t * rows : (t + 1) * rows, :LANES]
+            if t:
+                right = wide[(t - 1) * rows : t * rows, LANES:]
+                tile = right if tile is None else tile + right
+            tiles.append(pltpu.roll(tile, HALO, 1))
+        left = lax.broadcasted_iota(jnp.int32, (rows, LANES), 1) < HALO
+        return [jnp.where(left, tiles[b], tiles[b + 1]) for b in range(blocks)]
 
     def part_copy(v, source, other):
         return remote(
-            part_send.at[v, other],
+            part_send.at[v, slot(other)],
             part_recv.at[v, source],
             part_ssem.at[v, other],
             part_rsem.at[v, source],
@@ -224,7 +309,7 @@
         )
 
     def far_copy(v, step, source):
-        other = far0 + step
+        other = (far_level + step) * 2 + column
         return remote(
             far_send.at[v, step],
             part_recv.at[v, source],
@@ -235,11 +320,11 @@
 
     def hop_copy(v):
         return remote(
-            part_send.at[v, pl.ds(far0, half)],
+            part_send.at[v, pl.ds((1 - column) * levels + far_level, near_levels)],
             hop_recv.at[v],
             hop_ssem.at[v],
             hop_rsem.at[v],
-            rail(partner),
+            rail(mate),
         )
 
     def like_copy(v, owner):
@@ -252,29 +337,27 @@
         )
 
     def forward(v):
-        @pl.when(inner == 1)
-        def _():
-            hop_copy(v).wait_recv()
-
-            @pl.loop(0, half)
-            def _(step):
-                total = far_own[v % 2, far0 + step] + hop_recv[v, step].astype(jnp.float32)
-                far_send[v, step] = total.astype(jnp.bfloat16)
-                far_copy(v, step, chip).start()
+        hop_copy(v).wait_recv()
+
+        @pl.loop(0, near_levels)
+        def _(step):
+            total = far_own[v, column * levels + far_level + step] + hop_recv[v, step].astype(jnp.float32)
+            far_send[v, step] = total.astype(jnp.bfloat16)
+            far_copy(v, step, chip).start()
 
     def finish_like(v):
         each_near(lambda other: part_copy(v, other, other).wait_recv())
 
-        @pl.loop(0, quarter)
+        @pl.loop(0, near_levels)
         def _(step):
-            far_copy(v, 0, far_inner + step).wait_recv()
-
-        near = part_recv[v, near0].astype(jnp.float32)
+            far_copy(v, 0, (far_level + step) * 2 + column).wait_recv()
+
+        near = far_own[v, slot(chip)]
         for step in range(1, half):
-            near = near + part_recv[v, near0 + step].astype(jnp.float32)
-        far = part_recv[v, far_inner].astype(jnp.float32)
-        for step in range(1, quarter):
-            far = far + part_recv[v, far_inner + step].astype(jnp.float32)
+            near = near + part_recv[v, near0 + lax.rem(chip - near0 + step, half)].astype(jnp.float32)
+        far = part_recv[v, far_level * 2 + column].astype(jnp.float32)
+        for step in range(1, near_levels):
+            far = far + part_recv[v, (far_level + step) * 2 + column].astype(jnp.float32)
         first_kind = near0 == 0
         signal = jnp.where(first_kind, near, far) / spline_norm
         weight = jnp.where(first_kind, far, near) / spline_norm
@@ -286,45 +369,45 @@
         def _():
             like_copy(v, chip).start()
 
-    late = 3
-
     @pl.loop(0, chips)
-    def _(v):
-        total = stack_one(
-            vel_all[v, 0, 0],
-            vel_all[v, 0, 1],
-            time,
-            padded,
-            bands,
-            rows_done,
-            2 * count,
-            rows,
-            cols,
-        )
-        for t in range(chips):
-            start = t % blocks * rows + t // blocks * slice_rows
-            piece = total[start : start + slice_rows]
-            far_own[v % 2, t] = piece
-            part_send[v, t] = piece.astype(jnp.bfloat16)
-        part_recv[v, chip] = part_send[v, chip]
-
-        @pl.when(inner == 0)
+    def _(i):
+        begun = (i + chips - 1) // chips
+        v = (i - 1 + (i - 1 - chip + chips) // chips) * begun + chip * (1 - begun)
+
+        @pl.when(i >= 1)
         def _():
-            hop_copy(v).start()
-
+            vel_copy(v, v, v).wait_recv()
+
+        total = stack(vel_all[v, 0, 0], vel_all[v, 0, 1])
+        for owner in range(chips):
+            start = owner // blocks * slice_rows
+            piece = total[owner % blocks][start : start + slice_rows]
+            at = owner % 2 * levels + owner // 2
+            far_own[v, at] = piece
+            part_send[v, at] = piece.astype(jnp.bfloat16)
+
+        hop_copy(v).start()
         each_near(lambda other: part_copy(v, chip, other).start())
 
-        @pl.when(v >= 1)
+        @pl.when(i >= FORWARD_LAG)
         def _():
-            forward(v - 1)
-
-        @pl.when(v >= late)
+            forward(i - FORWARD_LAG)
+
+        @pl.when(i >= LIKE_LAG)
         def _():
-            finish_like(v - late)
-
-    forward(chips - 1)
-
-    @pl.loop(chips - late, chips)
+            finish_like(i - LIKE_LAG)
+
+    gap = LIKE_LAG - FORWARD_LAG
+
+    @pl.loop(chips, chips + FORWARD_LAG)
+    def _(i):
+        forward(i - FORWARD_LAG)
+
+        @pl.when(i >= LIKE_LAG)
+        def _():
+            finish_like(i - LIKE_LAG)
+
+    @pl.loop(chips - gap, chips)
     def _(v):
         finish_like(v)
 
@@ -349,20 +432,16 @@
     @pl.loop(0, chips)
     def _(v):
         each_near(lambda other: part_copy(v, chip, other).wait_send())
-
-        @pl.when(inner == 0)
-        def _():
-            hop_copy(v).wait_send()
-
-        @pl.when(inner == 1)
-        def _():
-            @pl.loop(0, half)
-            def _(step):
-                far_copy(v, step, chip).wait_send()
+        hop_copy(v).wait_send()
+
+        @pl.loop(0, near_levels)
+        def _(step):
+            far_copy(v, step, chip).wait_send()
 
     swap.wait_send()
 
     def finish(other):
+        vel_copy(other, chip, other).wait_send()
         like_copy(other, other).wait()
         best_copy(other, other).wait()
 
@@ -373,8 +452,9 @@
     count, rows, cols = epoch_maps.shape
     epochs = slot_epoch.shape[0]
     chips = n // 2
-    half = chips // 2
-    slice_rows = rows * (cols // LANES) // chips
+    half, quarter = chips // 2, chips // 4
+    blocks = cols // LANES
+    slice_rows = rows * blocks // chips
     smem = pl.BlockSpec(memory_space=pltpu.SMEM)
     vmem = pl.BlockSpec(memory_space=pltpu.VMEM)
     f32, bf16 = jnp.float32, jnp.bfloat16
@@ -386,15 +466,17 @@
         out_specs=vmem,
         scratch_shapes=[
             pltpu.VMEM((count, rows, cols), bf16),
-            pltpu.VMEM((2 * count, rows, cols + 2 * HALO), bf16),
-            pltpu.VMEM((2 * count * 2 * LANES, LANES), bf16),
-            pltpu.VMEM((2 * count, rows, cols + 2 * HALO), bf16),
+            pltpu.VMEM((4 * (rows + 2 * EDGE), rows), bf16),
+            pltpu.VMEM((2 * count * 4, blocks, rows + 2 * REACH, LANES), f32),
+            pltpu.VMEM((4, 2, LANES + 2 * REACH, LANES), f32),
+            pltpu.VMEM((blocks * rows, 2 * count * LANES), bf16),
+            pltpu.VMEM((2 * count * LANES, 2 * LANES), bf16),
             pltpu.SMEM((chips, 1, 2), jnp.int32),
             pltpu.VMEM((chips, chips, slice_rows, LANES), bf16),
             pltpu.VMEM((chips, chips, slice_rows, LANES), bf16),
-            pltpu.VMEM((2, chips, slice_rows, LANES), f32),
-            pltpu.VMEM((chips, half, slice_rows, LANES), bf16),
-            pltpu.VMEM((chips, half, slice_rows, LANES), bf16),
+            pltpu.VMEM((chips, chips, slice_rows, LANES), f32),
+            pltpu.VMEM((chips, quarter, slice_rows, LANES), bf16),
+            pltpu.VMEM((chips, quarter, slice_rows, LANES), bf16),
             pltpu.VMEM((chips, slice_rows, LANES), f32),
             pltpu.VMEM((slice_rows, LANES), f32),
             pltpu.VMEM((slice_rows, LANES), f32),

time: 45.7 us -> 40.7 us (0.89)
  Pallas kernels: 43.2 us -> 38.2 us
    pallas_call x1, Pallas kernels: 43.2 us -> 38.2 us  [fused(): pl.pallas_call(functools.partial(fused_kernel, chips, epochs, count, rows...]
where the time goes in v1:
time: 40.7 us; the launch traced here: 40.6 us
  Pallas kernels  38.2 us (94%)
  local copies, waits for them, and re-layouts  1.79 us (4%)
  between operations  0.64 us (2%)
    pallas_call x1, Pallas kernels, fused(): pl.pallas_call(functools.partial(fused_kernel, chips, epochs, count, rows...  38.2 us
    squeeze x1, local copies, waits for them, and re-layouts, fused(): return (both[:1], both[1])  1.79 us

profile of v1, /device:TPU:0, one launch (start us, length us, event | category | flops | bytes accessed | tf_op | source)
XLA Modules:
  0.0 40.6 jit_solution(1658836290224091465)
XLA Ops:
  0.6 38.2 %shard_map.59 = f32[2,96,512]{2,1,0:T(8,128)} custom-call(s32[64]{0:T(128)} %se_ref.1, s32[64]{0:T(128)} %et_ref.1, s32[1,2]{1,0:T(1,128)} %vel_ref.1, bf16[8,96,512]{2,1,0:T(8,128)(2,1)} %images.1), custom_call_target="tpu_custom_call" | custom-call | tf_op jit(solution)/shard_map/pallas_call | solution.py:462
  38.8 1.8 %slice_bitcast_fusion = (f32[96,512]{1,0:T(8,128)}, f32[1,96,512]{2,1,0:T(8,128)}) fusion(f32[2,96,512]{2,1,0:T(8,128)} %shard_map.59), kind=kLoop, calls=%fused_computation | loop fusion | bytes 786432 | tf_op jit(solution)/shard_map/squeeze | solution.py:499

commit v2 on v1

--- a/solution.py
+++ b/solution.py
@@ -20,8 +20,8 @@
 LANES = 128
 REACH = 16
 EDGE = 8
-FORWARD_LAG = 3
-LIKE_LAG = 6
+FIT_PIXELS = 1 << 19
+FORWARD_LAG = 4
 
 
 def scalar_taps(offset):
@@ -134,20 +134,22 @@
     vel_all,
     part_send,
     part_recv,
-    far_own,
-    hop_recv,
+    own,
     far_send,
+    far_recv,
     like_send,
-    max_send,
+    best_mine,
     max_recv,
+    cross_send,
+    cross_recv,
     best_send,
     image_sems,
     vel_send,
     vel_recv,
     part_ssem,
     part_rsem,
-    hop_ssem,
-    hop_rsem,
+    far_ssem,
+    far_rsem,
     max_sems,
     like_ssem,
     like_rsem,
@@ -159,23 +161,25 @@
     chip, core = me // 2, me % 2
     sibling = chip * 2 + 1 - core
     blocks = cols // LANES
-    levels, near_levels = chips // 2, chips // 4
+    near_levels = chips // 4
     half = chips // 2
-    slice_rows = rows * blocks // chips
-    level, column = chip // 2, chip % 2
-    mate = level * 2 + 1 - column
-    near0 = level // near_levels * half
-    far_level = near_levels - level // near_levels * near_levels
+    slice_rows = rows * blocks // half
+    share_rows = slice_rows // 2
+    near0 = chip // half * half
+    far0 = half - near0
+    place = chip - near0
     images_all = 2 * count
 
-    def window(owner):
+    def slot(owner):
+        return owner % 2 * near_levels + owner // 2 % near_levels
+
+    def window(owner, begin, size):
+        at = slot(owner)
+        start = at // blocks * slice_rows + begin
         return (
-            pl.ds(pl.multiple_of(owner // blocks * slice_rows, slice_rows), slice_rows),
-            pl.ds(pl.multiple_of(owner % blocks * LANES, LANES), LANES),
-        )
-
-    def slot(owner):
-        return owner % 2 * levels + owner // 2
+            pl.ds(pl.multiple_of(start, share_rows), size),
+            pl.ds(pl.multiple_of(at % blocks * LANES, LANES), LANES),
+        )
 
     def remote(source, target, send, receive, device):
         return pltpu.make_async_remote_copy(
@@ -208,6 +212,7 @@
     barrier = pltpu.get_barrier_semaphore()
     greet(sibling)
     each_rail(lambda other: greet(rail(other)))
+    each_near(lambda other: greet(other * 2 + 1 - core))
 
     span = rows + 2 * EDGE
     relative = (
@@ -245,8 +250,8 @@
     def _(s):
         filter_rows(images, s, s)
 
-    max_send[...] = jnp.full_like(max_send, -jnp.inf)
-    pl.semaphore_wait(barrier, chips)
+    best_mine[...] = jnp.full_like(best_mine, -jnp.inf)
+    pl.semaphore_wait(barrier, chips + half - 1)
 
     def vel_copy(source, target, other):
         return remote(vel_ref, vel_all.at[target], vel_send.at[source], vel_recv.at[target], rail(other))
@@ -302,159 +307,145 @@
     def part_copy(v, source, other):
         return remote(
             part_send.at[v, slot(other)],
-            part_recv.at[v, source],
-            part_ssem.at[v, other],
-            part_rsem.at[v, source],
+            part_recv.at[v, source - near0],
+            part_ssem.at[v, other - near0],
+            part_rsem.at[v, source - near0],
             rail(other),
         )
 
-    def far_copy(v, step, source):
-        other = (far_level + step) * 2 + column
+    def far_copy(f):
         return remote(
-            far_send.at[v, step],
-            part_recv.at[v, source],
-            part_ssem.at[v, other],
-            part_rsem.at[v, source],
-            rail(other),
-        )
-
-    def hop_copy(v):
+            far_send.at[f], far_recv.at[f], far_ssem.at[f], far_rsem.at[f], rail(far0 + place)
+        )
+
+    def like_copy(o, owner):
+        where = window(owner, 0, slice_rows)
         return remote(
-            part_send.at[v, pl.ds((1 - column) * levels + far_level, near_levels)],
-            hop_recv.at[v],
-            hop_ssem.at[v],
-            hop_rsem.at[v],
-            rail(mate),
-        )
-
-    def like_copy(v, owner):
-        return remote(
-            like_send.at[v],
-            like_out.at[0, window(owner)[0], window(owner)[1]],
-            like_ssem.at[v],
+            like_send.at[o],
+            like_out.at[0, where[0], where[1]],
+            like_ssem.at[o],
             like_rsem.at[owner],
-            rail(v),
-        )
-
-    def forward(v):
-        hop_copy(v).wait_recv()
-
-        @pl.loop(0, near_levels)
-        def _(step):
-            total = far_own[v, column * levels + far_level + step] + hop_recv[v, step].astype(jnp.float32)
-            far_send[v, step] = total.astype(jnp.bfloat16)
-            far_copy(v, step, chip).start()
-
-    def finish_like(v):
+            rail(near0 + o),
+        )
+
+    def near_sum(v):
         each_near(lambda other: part_copy(v, other, other).wait_recv())
-
-        @pl.loop(0, near_levels)
-        def _(step):
-            far_copy(v, 0, (far_level + step) * 2 + column).wait_recv()
-
-        near = far_own[v, slot(chip)]
+        total = own[v, slot(chip)]
         for step in range(1, half):
-            near = near + part_recv[v, near0 + lax.rem(chip - near0 + step, half)].astype(jnp.float32)
-        far = part_recv[v, far_level * 2 + column].astype(jnp.float32)
-        for step in range(1, near_levels):
-            far = far + part_recv[v, (far_level + step) * 2 + column].astype(jnp.float32)
+            total = total + part_recv[v, lax.rem(place + step, half)].astype(jnp.float32)
+        return total
+
+    def forward(f):
+        far_send[f] = near_sum(far0 + f).astype(jnp.bfloat16)
+        far_copy(f).start()
+
+    def finish_like(o):
+        near = near_sum(near0 + o)
+        far_copy(o).wait_recv()
+        far = far_recv[o].astype(jnp.float32)
         first_kind = near0 == 0
         signal = jnp.where(first_kind, near, far) / spline_norm
         weight = jnp.where(first_kind, far, near) / spline_norm
         value = signal / jnp.sqrt(weight + 1.0)
-        max_send[...] = jnp.maximum(max_send[...], value)
-        like_send[v] = value
-
-        @pl.when(v != chip)
+        best_mine[...] = jnp.maximum(best_mine[...], value)
+        like_send[o] = value
+
+        @pl.when(o != place)
         def _():
-            like_copy(v, chip).start()
+            like_copy(o, chip).start()
 
     @pl.loop(0, chips)
     def _(i):
         begun = (i + chips - 1) // chips
-        v = (i - 1 + (i - 1 - chip + chips) // chips) * begun + chip * (1 - begun)
+        later = (i - 1 - half + chips) // chips
+        turn = (i - 1 - half) * later
+        near_v = near0 + (turn + (turn - place + half) // half) * later + place * (1 - begun)
+        is_far = begun - later
+        v = is_far * (far0 + i - 1) + (1 - is_far) * near_v
 
         @pl.when(i >= 1)
         def _():
             vel_copy(v, v, v).wait_recv()
 
         total = stack(vel_all[v, 0, 0], vel_all[v, 0, 1])
-        for owner in range(chips):
-            start = owner // blocks * slice_rows
-            piece = total[owner % blocks][start : start + slice_rows]
-            at = owner % 2 * levels + owner // 2
-            far_own[v, at] = piece
+        for at in range(half):
+            start = at // blocks * slice_rows
+            piece = total[at % blocks][start : start + slice_rows]
+            own[v, at] = piece
             part_send[v, at] = piece.astype(jnp.bfloat16)
 
-        hop_copy(v).start()
         each_near(lambda other: part_copy(v, chip, other).start())
 
-        @pl.when(i >= FORWARD_LAG)
+        @pl.when(i >= 1 + FORWARD_LAG)
         def _():
-            forward(i - FORWARD_LAG)
-
-        @pl.when(i >= LIKE_LAG)
-        def _():
-            finish_like(i - LIKE_LAG)
-
-    gap = LIKE_LAG - FORWARD_LAG
-
-    @pl.loop(chips, chips + FORWARD_LAG)
-    def _(i):
-        forward(i - FORWARD_LAG)
-
-        @pl.when(i >= LIKE_LAG)
-        def _():
-            finish_like(i - LIKE_LAG)
-
-    @pl.loop(chips - gap, chips)
-    def _(v):
-        finish_like(v)
-
-    meet = remote(max_send, max_recv, max_sems.at[0], max_sems.at[1], sibling)
+            forward(i - 1 - FORWARD_LAG)
+
+    @pl.loop(chips - 1 - FORWARD_LAG, half)
+    def _(f):
+        forward(f)
+
+    @pl.loop(0, half)
+    def _(o):
+        finish_like(o)
+
+    other_core = 1 - core
+    mine = pl.ds(pl.multiple_of(core * share_rows, share_rows), share_rows)
+    theirs = pl.ds(pl.multiple_of(other_core * share_rows, share_rows), share_rows)
+    meet = remote(best_mine.at[theirs], max_recv, max_sems.at[0], max_sems.at[1], sibling)
     meet.start()
-    like_out[0, window(chip)[0], window(chip)[1]] = like_send[chip]
-    meet.wait()
-    best_send[...] = jnp.maximum(max_send[...], max_recv[...])
-
-    def best_copy(owner, other):
+    where = window(chip, 0, slice_rows)
+    like_out[0, where[0], where[1]] = like_send[place]
+    meet.wait_recv()
+    cross_send[...] = jnp.maximum(best_mine[mine, :], max_recv[...])
+    cross = remote(cross_send, cross_recv, max_sems.at[2], max_sems.at[3], rail(far0 + place))
+    cross.start()
+    cross.wait_recv()
+    best_send[...] = jnp.maximum(cross_send[...], cross_recv[...])
+
+    def best_copy(source, target):
+        where = window(source // 2, source % 2 * share_rows, share_rows)
         return remote(
             best_send,
-            best_out.at[window(owner)[0], window(owner)[1]],
-            best_ssem.at[other],
-            best_rsem.at[owner],
-            rail(other),
-        )
-
-    each_rail(lambda other: best_copy(chip, other).start())
-    best_out[window(chip)[0], window(chip)[1]] = best_send[...]
+            best_out.at[where[0], where[1]],
+            best_ssem.at[target],
+            best_rsem.at[source],
+            near0 * 2 + target,
+        )
+
+    seat = place * 2 + core
+
+    def each_seat(body):
+        @pl.loop(1, 2 * half)
+        def _(step):
+            body(lax.rem(seat + step, 2 * half))
+
+    each_seat(lambda target: best_copy(seat, target).start())
+    where = window(chip, core * share_rows, share_rows)
+    best_out[where[0], where[1]] = best_send[...]
 
     @pl.loop(0, chips)
     def _(v):
         each_near(lambda other: part_copy(v, chip, other).wait_send())
-        hop_copy(v).wait_send()
-
-        @pl.loop(0, near_levels)
-        def _(step):
-            far_copy(v, step, chip).wait_send()
+
+    @pl.loop(0, half)
+    def _(f):
+        far_copy(f).wait_send()
 
     swap.wait_send()
-
-    def finish(other):
-        vel_copy(other, chip, other).wait_send()
-        like_copy(other, other).wait()
-        best_copy(other, other).wait()
-
-    each_rail(finish)
+    meet.wait_send()
+    cross.wait_send()
+    each_rail(lambda other: vel_copy(other, chip, other).wait_send())
+    each_near(lambda other: like_copy(other - near0, other).wait())
+    each_seat(lambda other: best_copy(other, other).wait())
 
 
 def fused(n, epoch_maps, velocity, slot_epoch, epoch_time):
     count, rows, cols = epoch_maps.shape
     epochs = slot_epoch.shape[0]
     chips = n // 2
-    half, quarter = chips // 2, chips // 4
+    half = chips // 2
     blocks = cols // LANES
-    slice_rows = rows * blocks // chips
+    slice_rows = rows * blocks // half
     smem = pl.BlockSpec(memory_space=pltpu.SMEM)
     vmem = pl.BlockSpec(memory_space=pltpu.VMEM)
     f32, bf16 = jnp.float32, jnp.bfloat16
@@ -472,27 +463,29 @@
             pltpu.VMEM((blocks * rows, 2 * count * LANES), bf16),
             pltpu.VMEM((2 * count * LANES, 2 * LANES), bf16),
             pltpu.SMEM((chips, 1, 2), jnp.int32),
-            pltpu.VMEM((chips, chips, slice_rows, LANES), bf16),
-            pltpu.VMEM((chips, chips, slice_rows, LANES), bf16),
-            pltpu.VMEM((chips, chips, slice_rows, LANES), f32),
-            pltpu.VMEM((chips, quarter, slice_rows, LANES), bf16),
-            pltpu.VMEM((chips, quarter, slice_rows, LANES), bf16),
-            pltpu.VMEM((chips, slice_rows, LANES), f32),
+            pltpu.VMEM((chips, half, slice_rows, LANES), bf16),
+            pltpu.VMEM((chips, half, slice_rows, LANES), bf16),
+            pltpu.VMEM((chips, half, slice_rows, LANES), f32),
+            pltpu.VMEM((half, slice_rows, LANES), bf16),
+            pltpu.VMEM((half, slice_rows, LANES), bf16),
+            pltpu.VMEM((half, slice_rows, LANES), f32),
             pltpu.VMEM((slice_rows, LANES), f32),
-            pltpu.VMEM((slice_rows, LANES), f32),
-            pltpu.VMEM((slice_rows, LANES), f32),
+            pltpu.VMEM((slice_rows // 2, LANES), f32),
+            pltpu.VMEM((slice_rows // 2, LANES), f32),
+            pltpu.VMEM((slice_rows // 2, LANES), f32),
+            pltpu.VMEM((slice_rows // 2, LANES), f32),
             dma((2,)),
             dma((chips,)),
             dma((chips,)),
-            dma((chips, chips)),
-            dma((chips, chips)),
+            dma((chips, half)),
+            dma((chips, half)),
+            dma((half,)),
+            dma((half,)),
+            dma((4,)),
+            dma((half,)),
             dma((chips,)),
-            dma((chips,)),
-            dma((2,)),
-            dma((chips,)),
-            dma((chips,)),
-            dma((chips,)),
-            dma((chips,)),
+            dma((2 * half,)),
+            dma((2 * half,)),
         ],
         compiler_params=pltpu.CompilerParams(collective_id=0, has_side_effects=True),
     )(slot_epoch, epoch_time, velocity, epoch_maps)
@@ -504,12 +497,13 @@
     chips = n // 2
     blocks = cols // LANES
     return (
-        n % 4 == 0
+        n % 8 == 0
         and velocity.shape[0] == 1
         and n * count == 2 * epochs
         and cols % LANES == 0
-        and chips % blocks == 0
-        and rows % (chips // blocks * 16) == 0
+        and chips // 2 % blocks == 0
+        and rows % (chips // 2 // blocks * 16) == 0
+        and rows * cols * count <= FIT_PIXELS
     )
 
 

time: 40.7 us -> 36.7 us (0.902)
  Pallas kernels: 38.2 us -> 34.1 us
    pallas_call x1, Pallas kernels: 38.2 us -> 34.1 us  [fused(): pl.pallas_call(functools.partial(fused_kernel, chips, epochs, count, rows...]
where the time goes in v2:
time: 36.7 us; the launch traced here: 36.6 us
  Pallas kernels  34.1 us (93%)
  local copies, waits for them, and re-layouts  1.79 us (5%)
  between operations  0.64 us (2%)
    pallas_call x1, Pallas kernels, fused(): pl.pallas_call(functools.partial(fused_kernel, chips, epochs, count, rows...  34.1 us
    squeeze x1, local copies, waits for them, and re-layouts, fused(): return (both[:1], both[1])  1.79 us

profile of v2, /device:TPU:0, one launch (start us, length us, event | category | flops | bytes accessed | tf_op | source)
XLA Modules:
  0.0 36.6 jit_solution(9726175231554313607)
XLA Ops:
  0.6 34.1 %shard_map.59 = f32[2,96,512]{2,1,0:T(8,128)} custom-call(s32[64]{0:T(128)} %se_ref.1, s32[64]{0:T(128)} %et_ref.1, s32[1,2]{1,0:T(1,128)} %vel_ref.1, bf16[8,96,512]{2,1,0:T(8,128)(2,1)} %images.1), custom_call_target="tpu_custom_call" | custom-call | tf_op jit(solution)/shard_map/pallas_call | solution.py:453
  34.8 1.8 %slice_bitcast_fusion = (f32[96,512]{1,0:T(8,128)}, f32[1,96,512]{2,1,0:T(8,128)}) fusion(f32[2,96,512]{2,1,0:T(8,128)} %shard_map.59), kind=kLoop, calls=%fused_computation | loop fusion | bytes 786432 | tf_op jit(solution)/shard_map/squeeze | solution.py:492

commit v3 on v2

--- a/solution.py
+++ b/solution.py
@@ -120,11 +120,15 @@
     count,
     rows,
     cols,
+    se_in,
+    et_in,
+    vel_in,
+    maps,
+    out_ref,
     se_ref,
     et_ref,
     vel_ref,
     images,
-    out_ref,
     peer_images,
     row_taps,
     table,
@@ -143,7 +147,10 @@
     cross_send,
     cross_recv,
     best_send,
-    image_sems,
+    load_sems,
+    own_sems,
+    swap_ssem,
+    swap_rsem,
     vel_send,
     vel_recv,
     part_ssem,
@@ -209,10 +216,22 @@
             barrier, inc=1, device_id={"vel": device}, device_id_type=pl.DeviceIdType.MESH
         )
 
+    early = count // 2
+    loads = [
+        pltpu.make_async_copy(maps.at[pl.ds(0, early)], images.at[pl.ds(0, early)], load_sems.at[0]),
+        pltpu.make_async_copy(
+            maps.at[pl.ds(early, count - early)], images.at[pl.ds(early, count - early)], load_sems.at[1]
+        ),
+        pltpu.make_async_copy(vel_in, vel_ref, load_sems.at[2]),
+        pltpu.make_async_copy(se_in, se_ref, load_sems.at[3]),
+        pltpu.make_async_copy(et_in, et_ref, load_sems.at[4]),
+    ]
     barrier = pltpu.get_barrier_semaphore()
     greet(sibling)
     each_rail(lambda other: greet(rail(other)))
     each_near(lambda other: greet(other * 2 + 1 - core))
+    for load in loads:
+        load.start()
 
     span = rows + 2 * EDGE
     relative = (
@@ -244,20 +263,27 @@
                     f * span : (f + 1) * span, b * LANES : (b + 1) * LANES
                 ]
 
-    early = count // 2
+    loads[0].wait()
 
     @pl.loop(0, early)
     def _(s):
         filter_rows(images, s, s)
 
     best_mine[...] = jnp.full_like(best_mine, -jnp.inf)
+    for load in loads[1:]:
+        load.wait()
     pl.semaphore_wait(barrier, chips + half - 1)
 
     def vel_copy(source, target, other):
         return remote(vel_ref, vel_all.at[target], vel_send.at[source], vel_recv.at[target], rail(other))
 
-    swap = remote(images, peer_images, image_sems.at[0], image_sems.at[1], sibling)
-    swap.start()
+    def swap(s):
+        return remote(images.at[s], peer_images.at[s], swap_ssem.at[s], swap_rsem.at[s], sibling)
+
+    @pl.loop(0, count)
+    def _(s):
+        swap(s).start()
+
     each_rail(lambda other: vel_copy(other, chip, other).start())
     vel_all[chip, 0, 0] = vel_ref[0, 0]
     vel_all[chip, 0, 1] = vel_ref[0, 1]
@@ -266,10 +292,9 @@
     def _(s):
         filter_rows(images, s, s)
 
-    swap.wait_recv()
-
     @pl.loop(0, count)
     def _(s):
+        swap(s).wait_recv()
         filter_rows(peer_images, s, s + count)
 
     first = lax.rem(me * count, epochs)
@@ -350,10 +375,6 @@
         best_mine[...] = jnp.maximum(best_mine[...], value)
         like_send[o] = value
 
-        @pl.when(o != place)
-        def _():
-            like_copy(o, chip).start()
-
     @pl.loop(0, chips)
     def _(i):
         begun = (i + chips - 1) // chips
@@ -393,12 +414,18 @@
     theirs = pl.ds(pl.multiple_of(other_core * share_rows, share_rows), share_rows)
     meet = remote(best_mine.at[theirs], max_recv, max_sems.at[0], max_sems.at[1], sibling)
     meet.start()
-    where = window(chip, 0, slice_rows)
-    like_out[0, where[0], where[1]] = like_send[place]
     meet.wait_recv()
     cross_send[...] = jnp.maximum(best_mine[mine, :], max_recv[...])
     cross = remote(cross_send, cross_recv, max_sems.at[2], max_sems.at[3], rail(far0 + place))
     cross.start()
+    each_near(lambda other: like_copy(other - near0, chip).start())
+    where = window(chip, 0, slice_rows)
+    keeps = [
+        pltpu.make_async_copy(
+            like_send.at[place], like_out.at[0, where[0], where[1]], own_sems.at[0]
+        )
+    ]
+    keeps[0].start()
     cross.wait_recv()
     best_send[...] = jnp.maximum(cross_send[...], cross_recv[...])
 
@@ -421,7 +448,10 @@
 
     each_seat(lambda target: best_copy(seat, target).start())
     where = window(chip, core * share_rows, share_rows)
-    best_out[where[0], where[1]] = best_send[...]
+    keeps.append(
+        pltpu.make_async_copy(best_send, best_out.at[where[0], where[1]], own_sems.at[1])
+    )
+    keeps[1].start()
 
     @pl.loop(0, chips)
     def _(v):
@@ -431,7 +461,12 @@
     def _(f):
         far_copy(f).wait_send()
 
-    swap.wait_send()
+    @pl.loop(0, count)
+    def _(s):
+        swap(s).wait_send()
+
+    for keep in keeps:
+        keep.wait()
     meet.wait_send()
     cross.wait_send()
     each_rail(lambda other: vel_copy(other, chip, other).wait_send())
@@ -446,16 +481,19 @@
     half = chips // 2
     blocks = cols // LANES
     slice_rows = rows * blocks // half
-    smem = pl.BlockSpec(memory_space=pltpu.SMEM)
-    vmem = pl.BlockSpec(memory_space=pltpu.VMEM)
+    whole = pl.BlockSpec(memory_space=pl.ANY)
     f32, bf16 = jnp.float32, jnp.bfloat16
     dma = pltpu.SemaphoreType.DMA
     both = pl.pallas_call(
         functools.partial(fused_kernel, chips, epochs, count, rows, cols),
         out_shape=jax.ShapeDtypeStruct((2, rows, cols), f32),
-        in_specs=[smem, smem, smem, vmem],
-        out_specs=vmem,
+        in_specs=[whole] * 4,
+        out_specs=whole,
         scratch_shapes=[
+            pltpu.SMEM((epochs,), jnp.int32),
+            pltpu.SMEM((epochs,), jnp.int32),
+            pltpu.SMEM((1, 2), jnp.int32),
+            pltpu.VMEM((count, rows, cols), bf16),
             pltpu.VMEM((count, rows, cols), bf16),
             pltpu.VMEM((4 * (rows + 2 * EDGE), rows), bf16),
             pltpu.VMEM((2 * count * 4, blocks, rows + 2 * REACH, LANES), f32),
@@ -474,7 +512,10 @@
             pltpu.VMEM((slice_rows // 2, LANES), f32),
             pltpu.VMEM((slice_rows // 2, LANES), f32),
             pltpu.VMEM((slice_rows // 2, LANES), f32),
+            dma((5,)),
             dma((2,)),
+            dma((count,)),
+            dma((count,)),
             dma((chips,)),
             dma((chips,)),
             dma((chips, half)),

time: 36.7 us -> 34.8 us (0.948)
  Pallas kernels: 34.1 us -> 32.2 us
    pallas_call x1, Pallas kernels: 34.1 us -> 32.2 us  [fused(): pl.pallas_call(functools.partial(fused_kernel, chips, epochs, count, rows...]
where the time goes in v3:
time: 34.8 us; the launch traced here: 34.6 us
  Pallas kernels  32.2 us (93%)
  local copies, waits for them, and re-layouts  1.79 us (5%)
  between operations  0.64 us (2%)
    pallas_call x1, Pallas kernels, fused(): pl.pallas_call(functools.partial(fused_kernel, chips, epochs, count, rows...  32.2 us
    squeeze x1, local copies, waits for them, and re-layouts, fused(): return (both[:1], both[1])  1.79 us

profile of v3, /device:TPU:0, one launch (start us, length us, event | category | flops | bytes accessed | tf_op | source)
XLA Modules:
  0.0 34.6 jit_solution(17383914519263302102)
XLA Ops:
  0.6 32.2 %shard_map.59 = f32[2,96,512]{2,1,0:T(8,128)} custom-call(s32[64]{0:T(128)} %se_in.1, s32[64]{0:T(128)} %et_in.1, s32[1,2]{1,0:T(1,128)} %vel_in.1, bf16[8,96,512]{2,1,0:T(8,128)(2,1)} %maps.1), custom_call_target="tpu_custom_call" | custom-call | tf_op jit(solution)/shard_map/pallas_call | solution.py:487
  32.9 1.8 %slice_bitcast_fusion = (f32[96,512]{1,0:T(8,128)}, f32[1,96,512]{2,1,0:T(8,128)}) fusion(f32[2,96,512]{2,1,0:T(8,128)} %shard_map.59), kind=kLoop, calls=%fused_computation | loop fusion | bytes 786432 | tf_op jit(solution)/shard_map/squeeze | solution.py:533

commit v4 on v3

--- a/solution.py
+++ b/solution.py
@@ -133,8 +133,6 @@
     row_taps,
     table,
     base,
-    lhs,
-    bands,
     vel_all,
     part_send,
     part_recv,
@@ -143,9 +141,7 @@
     far_recv,
     like_send,
     best_mine,
-    max_recv,
-    cross_send,
-    cross_recv,
+    meet_recv,
     best_send,
     load_sems,
     own_sems,
@@ -157,7 +153,8 @@
     part_rsem,
     far_ssem,
     far_rsem,
-    max_sems,
+    meet_ssem,
+    meet_rsem,
     like_ssem,
     like_rsem,
     best_ssem,
@@ -230,6 +227,7 @@
     greet(sibling)
     each_rail(lambda other: greet(rail(other)))
     each_near(lambda other: greet(other * 2 + 1 - core))
+    greet((far0 + place) * 2 + 1 - core)
     for load in loads:
         load.start()
 
@@ -265,14 +263,15 @@
 
     loads[0].wait()
 
-    @pl.loop(0, early)
+    @pl.loop(0, early, step=2)
     def _(s):
         filter_rows(images, s, s)
+        filter_rows(images, s + 1, s + 1)
 
     best_mine[...] = jnp.full_like(best_mine, -jnp.inf)
     for load in loads[1:]:
         load.wait()
-    pl.semaphore_wait(barrier, chips + half - 1)
+    pl.semaphore_wait(barrier, chips + half)
 
     def vel_copy(source, target, other):
         return remote(vel_ref, vel_all.at[target], vel_send.at[source], vel_recv.at[target], rail(other))
@@ -288,14 +287,17 @@
     vel_all[chip, 0, 0] = vel_ref[0, 0]
     vel_all[chip, 0, 1] = vel_ref[0, 1]
 
-    @pl.loop(early, count)
+    @pl.loop(early, count, step=2)
     def _(s):
         filter_rows(images, s, s)
-
-    @pl.loop(0, count)
+        filter_rows(images, s + 1, s + 1)
+
+    @pl.loop(0, count, step=2)
     def _(s):
         swap(s).wait_recv()
+        swap(s + 1).wait_recv()
         filter_rows(peer_images, s, s + count)
+        filter_rows(peer_images, s + 1, s + 1 + count)
 
     first = lax.rem(me * count, epochs)
     peer_first = lax.rem(sibling * count, epochs)
@@ -305,18 +307,31 @@
         return et_ref[se_ref[at]]
 
     def stack(rate_row, rate_col):
+        shifted, weights = [], []
         for s in range(images_all):
             qr = (rate_row * time(s)) >> 5
             qc = (rate_col * time(s)) >> 5
-            for b in range(blocks):
-                lhs[b * rows : (b + 1) * rows, s * LANES : (s + 1) * LANES] = table[
-                    s * 4 + (qr & 3), b, pl.ds((qr >> 2) + REACH, rows), :
-                ].astype(jnp.bfloat16)
-            for h in range(2):
-                bands[s * LANES : (s + 1) * LANES, h * LANES : (h + 1) * LANES] = base[
-                    qc & 3, h, pl.ds(REACH - (qc >> 2), LANES), :
-                ].astype(jnp.bfloat16)
-        wide = jnp.dot(lhs[...], bands[...], preferred_element_type=jnp.float32)
+            shifted.append([
+                table[s * 4 + (qr & 3), b, pl.ds((qr >> 2) + REACH, rows), :].astype(jnp.bfloat16)
+                for b in range(blocks)
+            ])
+            weights.append(
+                jnp.concatenate(
+                    [
+                        base[qc & 3, h, pl.ds(REACH - (qc >> 2), LANES), :].astype(jnp.bfloat16)
+                        for h in range(2)
+                    ],
+                    axis=1,
+                )
+            )
+        lhs_all = jnp.concatenate(
+            [
+                jnp.concatenate([shifted[s][b] for s in range(images_all)], axis=1)
+                for b in range(blocks)
+            ],
+            axis=0,
+        )
+        wide = jnp.dot(lhs_all, jnp.concatenate(weights, axis=0), preferred_element_type=jnp.float32)
         tiles = []
         for t in range(blocks + 1):
             tile = None
@@ -412,12 +427,16 @@
     other_core = 1 - core
     mine = pl.ds(pl.multiple_of(core * share_rows, share_rows), share_rows)
     theirs = pl.ds(pl.multiple_of(other_core * share_rows, share_rows), share_rows)
-    meet = remote(best_mine.at[theirs], max_recv, max_sems.at[0], max_sems.at[1], sibling)
-    meet.start()
-    meet.wait_recv()
-    cross_send[...] = jnp.maximum(best_mine[mine, :], max_recv[...])
-    cross = remote(cross_send, cross_recv, max_sems.at[2], max_sems.at[3], rail(far0 + place))
-    cross.start()
+    mirror = far0 + place
+    meets = [
+        remote(best_mine.at[theirs], meet_recv.at[0], meet_ssem.at[0], meet_rsem.at[0], sibling),
+        remote(best_mine.at[mine], meet_recv.at[1], meet_ssem.at[1], meet_rsem.at[1], rail(mirror)),
+        remote(
+            best_mine.at[theirs], meet_recv.at[2], meet_ssem.at[2], meet_rsem.at[2], mirror * 2 + other_core
+        ),
+    ]
+    for meet in (meets[1], meets[2], meets[0]):
+        meet.start()
     each_near(lambda other: like_copy(other - near0, chip).start())
     where = window(chip, 0, slice_rows)
     keeps = [
@@ -426,8 +445,10 @@
         )
     ]
     keeps[0].start()
-    cross.wait_recv()
-    best_send[...] = jnp.maximum(cross_send[...], cross_recv[...])
+    for meet in meets:
+        meet.wait_recv()
+    best = jnp.maximum(best_mine[mine, :], meet_recv[0])
+    best_send[...] = jnp.maximum(best, jnp.maximum(meet_recv[1], meet_recv[2]))
 
     def best_copy(source, target):
         where = window(source // 2, source % 2 * share_rows, share_rows)
@@ -467,8 +488,9 @@
 
     for keep in keeps:
         keep.wait()
-    meet.wait_send()
-    cross.wait_send()
+    for meet in meets:
+        meet.wait_send()
+
     each_rail(lambda other: vel_copy(other, chip, other).wait_send())
     each_near(lambda other: like_copy(other - near0, other).wait())
     each_seat(lambda other: best_copy(other, other).wait())
@@ -498,8 +520,6 @@
             pltpu.VMEM((4 * (rows + 2 * EDGE), rows), bf16),
             pltpu.VMEM((2 * count * 4, blocks, rows + 2 * REACH, LANES), f32),
             pltpu.VMEM((4, 2, LANES + 2 * REACH, LANES), f32),
-            pltpu.VMEM((blocks * rows, 2 * count * LANES), bf16),
-            pltpu.VMEM((2 * count * LANES, 2 * LANES), bf16),
             pltpu.SMEM((chips, 1, 2), jnp.int32),
             pltpu.VMEM((chips, half, slice_rows, LANES), bf16),
             pltpu.VMEM((chips, half, slice_rows, LANES), bf16),
@@ -508,9 +528,7 @@
             pltpu.VMEM((half, slice_rows, LANES), bf16),
             pltpu.VMEM((half, slice_rows, LANES), f32),
             pltpu.VMEM((slice_rows, LANES), f32),
-            pltpu.VMEM((slice_rows // 2, LANES), f32),
-            pltpu.VMEM((slice_rows // 2, LANES), f32),
-            pltpu.VMEM((slice_rows // 2, LANES), f32),
+            pltpu.VMEM((3, slice_rows // 2, LANES), f32),
             pltpu.VMEM((slice_rows // 2, LANES), f32),
             dma((5,)),
             dma((2,)),
@@ -522,7 +540,8 @@
             dma((chips, half)),
             dma((half,)),
             dma((half,)),
-            dma((4,)),
+            dma((3,)),
+            dma((3,)),
             dma((half,)),
             dma((chips,)),
             dma((2 * half,)),
@@ -539,6 +558,7 @@
     blocks = cols // LANES
     return (
         n % 8 == 0
+        and count % 4 == 0
         and velocity.shape[0] == 1
         and n * count == 2 * epochs
         and cols % LANES == 0

time: 34.8 us -> 33.6 us (0.966)
  Pallas kernels: 32.2 us -> 31 us
    pallas_call x1, Pallas kernels: 32.2 us -> 31 us  [fused(): pl.pallas_call(functools.partial(fused_kernel, chips, epochs, count, rows...]
where the time goes in v4:
time: 33.6 us; the launch traced here: 33.5 us
  Pallas kernels  31 us (92%)
  local copies, waits for them, and re-layouts  1.79 us (5%)
  between operations  0.64 us (2%)
    pallas_call x1, Pallas kernels, fused(): pl.pallas_call(functools.partial(fused_kernel, chips, epochs, count, rows...  31 us
    squeeze x1, local copies, waits for them, and re-layouts, fused(): return (both[:1], both[1])  1.79 us

profile of v4, /device:TPU:0, one launch (start us, length us, event | category | flops | bytes accessed | tf_op | source)
XLA Modules:
  0.0 33.5 jit_solution(3563954357183089553)
XLA Ops:
  0.6 31.0 %shard_map.59 = f32[2,96,512]{2,1,0:T(8,128)} custom-call(s32[64]{0:T(128)} %se_in.1, s32[64]{0:T(128)} %et_in.1, s32[1,2]{1,0:T(1,128)} %vel_in.1, bf16[8,96,512]{2,1,0:T(8,128)(2,1)} %maps.1), custom_call_target="tpu_custom_call" | custom-call | tf_op jit(solution)/shard_map/pallas_call | solution.py:509
  31.7 1.8 %slice_bitcast_fusion = (f32[96,512]{1,0:T(8,128)}, f32[1,96,512]{2,1,0:T(8,128)}) fusion(f32[2,96,512]{2,1,0:T(8,128)} %shard_map.59), kind=kLoop, calls=%fused_computation | loop fusion | bytes 786432 | tf_op jit(solution)/shard_map/squeeze | solution.py:552

commit v5 on v4

--- a/solution.py
+++ b/solution.py
@@ -262,14 +262,16 @@
                 ]
 
     loads[0].wait()
-
-    @pl.loop(0, early, step=2)
+    loads[1].wait()
+    ready = count * 3 // 4
+
+    @pl.loop(0, ready, step=2)
     def _(s):
         filter_rows(images, s, s)
         filter_rows(images, s + 1, s + 1)
 
     best_mine[...] = jnp.full_like(best_mine, -jnp.inf)
-    for load in loads[1:]:
+    for load in loads[2:]:
         load.wait()
     pl.semaphore_wait(barrier, chips + half)
 
@@ -287,17 +289,17 @@
     vel_all[chip, 0, 0] = vel_ref[0, 0]
     vel_all[chip, 0, 1] = vel_ref[0, 1]
 
-    @pl.loop(early, count, step=2)
+    @pl.loop(ready, count, step=2)
     def _(s):
         filter_rows(images, s, s)
         filter_rows(images, s + 1, s + 1)
 
-    @pl.loop(0, count, step=2)
+    @pl.loop(0, count, step=4)
     def _(s):
-        swap(s).wait_recv()
-        swap(s + 1).wait_recv()
-        filter_rows(peer_images, s, s + count)
-        filter_rows(peer_images, s + 1, s + 1 + count)
+        for j in range(4):
+            swap(s + j).wait_recv()
+        for j in range(4):
+            filter_rows(peer_images, s + j, s + j + count)
 
     first = lax.rem(me * count, epochs)
     peer_first = lax.rem(sibling * count, epochs)

time: 33.6 us -> 33.6 us (level)
  no operation moved by 1% of the time
where the time goes in v5:
time: 33.6 us; the launch traced here: 33.3 us
  Pallas kernels  30.9 us (92%)
  local copies, waits for them, and re-layouts  1.79 us (5%)
  between operations  0.64 us (2%)
    pallas_call x1, Pallas kernels, fused(): pl.pallas_call(functools.partial(fused_kernel, chips, epochs, count, rows...  30.9 us
    squeeze x1, local copies, waits for them, and re-layouts, fused(): return (both[:1], both[1])  1.79 us

profile of v5, /device:TPU:0, one launch (start us, length us, event | category | flops | bytes accessed | tf_op | source)
XLA Modules:
  0.0 33.3 jit_solution(2964348919879782464)
XLA Ops:
  0.6 30.9 %shard_map.59 = f32[2,96,512]{2,1,0:T(8,128)} custom-call(s32[64]{0:T(128)} %se_in.1, s32[64]{0:T(128)} %et_in.1, s32[1,2]{1,0:T(1,128)} %vel_in.1, bf16[8,96,512]{2,1,0:T(8,128)(2,1)} %maps.1), custom_call_target="tpu_custom_call" | custom-call | tf_op jit(solution)/shard_map/pallas_call | solution.py:511
  31.5 1.8 %slice_bitcast_fusion = (f32[96,512]{1,0:T(8,128)}, f32[1,96,512]{2,1,0:T(8,128)}) fusion(f32[2,96,512]{2,1,0:T(8,128)} %shard_map.59), kind=kLoop, calls=%fused_computation | loop fusion | bytes 786432 | tf_op jit(solution)/shard_map/squeeze | solution.py:554
